TPU v7x, 256 devices: a whole 4x4x8 slice. The times are simulated.
256 devices in a mesh: seq: 64 (over y, z, core), tab: 4 (over x).
Axes of the slice: x: 4, y: 4, z: 8, core: 2. Of those that a mesh axis runs over, the one named last changes fastest.
Arguments:
- cotangent: bfloat16 [65536, 2560], P('seq', 'tab'), may hold values from -6 to 6
- saved_value: bfloat16 [65536, 2560], P('seq', 'tab'), may hold values from -6 to 6
- gate_scale: float32 [65536], P('seq'), may hold values from 0.2 to 1
- conv_weight: float32 [4, 2560], P(None, 'tab'), may hold values from -3 to 3
- value_weight: bfloat16 [1280, 2560], P(None, 'tab'), may hold values from -0.25 to 0.25
- owner_ids: int32 [8, 65536, 1], P('tab', 'seq'), may hold values from 0 to 63; in each aligned block of 1024 rows (0 to 1023, 1024 to 2047, ..., all dimensions but the last counted through in order) at most 64 rows name the same one
- local_row: int32 [8, 65536], P('tab', 'seq'), may hold values from 0 to 511
- row_table: float32 [8, 32768, 160], P('tab', 'seq'), may hold values from -6 to 6
- moment_one: float32 [8, 32768, 160], P('tab', 'seq'), may hold values from -6 to 6
- moment_two: float32 [8, 32768, 160], P('tab', 'seq'), may hold values from 0.5 to 4
Outputs:
- new_table: float32 [8, 32768, 160], P('tab', 'seq')
- new_first: float32 [8, 32768, 160], P('tab', 'seq')
- new_second: float32 [8, 32768, 160], P('tab', 'seq')
Inputs may be any that keep to these rules, and one draw needn't show every extreme that they name: `owner_ids`: within each aligned block of 1024 tokens of one head (one device's tokens), no owner is named by more than 64 tokens; in some blocks one owner is named by exactly 64.
All inputs are finite; a program needn't handle non-finite values.
Results may differ from a plain program's by a relative error of at most 0.0029.
Values may be sent and summed in bfloat16 or wider, within the bound.
No kernel may reach another device: no remote copies, remote signals or barrier semaphores. Data moves between devices by JAX's collectives and lax.ppermute only.
A program may use at most 128 MiB of HBM per device.

v0:
```python
import jax
import jax.numpy as jnp
from jax import lax
from jax.sharding import PartitionSpec as P

beta_one = 0.9
beta_two = 0.95
learn_rate = 0.01
adam_steps = 10.0
epsilon = 1e-08


def from_behind(block, axis, distance):
    devices = range(lax.axis_size(axis))
    route = [(i - distance, i) for i in devices if i - distance in devices]
    return lax.ppermute(block, axis, route)


def causal_mix(context, conv_weight, length):
    mix_total = jnp.zeros((length, context.shape[1]), jnp.float32)
    for tap_index in range(4):
        row_start = 9 - 3 * tap_index
        mix_total = (
            mix_total + conv_weight[tap_index][None, :] * context[row_start : row_start + length]
        )
    return mix_total


def conv_adjoint(upstream, mixed_conv):
    squashed = jax.nn.sigmoid(mixed_conv)
    return upstream * squashed * (1.0 + mixed_conv * (1.0 - squashed))


def shards(
    cotangent,
    saved_value,
    gate_scale,
    conv_weight,
    value_weight,
    owner_ids,
    local_row,
    row_table,
    moment_one,
    moment_two,
):
    length = cotangent.shape[0]
    head_local = row_table.shape[0]
    table_rows = row_table.shape[1]
    head_dim = row_table.shape[2]
    own_width = head_local * head_dim
    peer_count = lax.axis_size("seq")
    count_cap = 4 * length // peer_count
    upstream = cotangent.astype(jnp.float32)
    value_rows = saved_value.astype(jnp.float32)
    prior_rows = from_behind(saved_value[length - 9 :], "seq", 1)
    context = jnp.concatenate([prior_rows.astype(jnp.float32), value_rows], axis=0)
    conv_grad = conv_adjoint(upstream, causal_mix(context, conv_weight, length))
    following = from_behind(conv_grad[:9], "seq", -1)
    extended = jnp.concatenate([conv_grad, following], axis=0)
    value_grad = upstream
    for tap_index in range(4):
        row_start = 3 * tap_index
        value_grad = (
            value_grad + conv_weight[tap_index][None, :] * extended[row_start : row_start + length]
        )
    scaled = (gate_scale[:, None] * value_grad).astype(jnp.bfloat16)
    full_term = lax.dot_general(
        value_weight, scaled, (((1,), (1,)), ((), ())), preferred_element_type=jnp.float32
    )
    summed = lax.psum(full_term, "tab")
    memory_grad = lax.dynamic_slice_in_dim(summed, lax.axis_index("tab") * own_width, own_width, 0)
    heads_grad = jnp.swapaxes(memory_grad.reshape(head_local, head_dim, length), 1, 2)
    owners = owner_ids[:, :, 0]
    position = jnp.arange(length, dtype=jnp.int32)
    earlier = position[None, :] < position[:, None]
    same_owner = owners[:, :, None] == owners[:, None, :]
    slot_rank = jnp.sum((same_owner & earlier[None]).astype(jnp.int32), axis=2)
    slot_index = owners * count_cap + slot_rank
    head_ids = jnp.broadcast_to(jnp.arange(head_local, dtype=jnp.int32)[:, None], slot_index.shape)
    send_grad = (
        jnp.zeros((head_local, peer_count * count_cap, head_dim), jnp.float32)
        .at[head_ids, slot_index]
        .set(heads_grad)
    )
    send_rows = (
        jnp.zeros((head_local, peer_count * count_cap), jnp.int32)
        .at[head_ids, slot_index]
        .set(local_row + 1)
    )
    send_grad = send_grad.reshape(head_local, peer_count, count_cap, head_dim)
    send_rows = send_rows.reshape(head_local, peer_count, count_cap)
    grads_in = lax.all_to_all(send_grad, "seq", split_axis=1, concat_axis=1, tiled=True)
    rows_in = lax.all_to_all(send_rows, "seq", split_axis=1, concat_axis=1, tiled=True)
    item_count = grads_in.shape[0]
    flat_rows = rows_in.reshape(item_count, -1) - 1
    flat_grads = grads_in.reshape(item_count, -1, head_dim)
    item_ids = jnp.broadcast_to(jnp.arange(item_count, dtype=jnp.int32)[:, None], flat_rows.shape)
    target = jnp.where(flat_rows < 0, table_rows, flat_rows)
    summed_rows = (
        jnp.zeros((item_count, table_rows, head_dim), jnp.float32)
        .at[item_ids, target]
        .add(flat_grads, mode="drop")
    )
    row_hits = (
        jnp.zeros((item_count, table_rows), jnp.int32).at[item_ids, target].add(1, mode="drop")
    )
    row_grad, row_hits = (summed_rows, row_hits)
    touched = (row_hits > 0)[:, :, None]
    first_next = beta_one * moment_one + (1.0 - beta_one) * row_grad
    second_next = beta_two * moment_two + (1.0 - beta_two) * row_grad * row_grad
    update = (
        first_next
        / (1.0 - beta_one**adam_steps)
        / (jnp.sqrt(second_next / (1.0 - beta_two**adam_steps)) + epsilon)
    )
    table_next = row_table - learn_rate * update
    return (
        jnp.where(touched, table_next, row_table),
        jnp.where(touched, first_next, moment_one),
        jnp.where(touched, second_next, moment_two),
    )


def solution(mesh):
    in_specs = (
        P("seq", "tab"),
        P("seq", "tab"),
        P("seq"),
        P(None, "tab"),
        P(None, "tab"),
        P("tab", "seq", None),
        P("tab", "seq"),
        P("tab", "seq", None),
        P("tab", "seq", None),
        P("tab", "seq", None),
    )
    out_specs = (P("tab", "seq", None), P("tab", "seq", None), P("tab", "seq", None))
    return jax.shard_map(shards, mesh=mesh, in_specs=in_specs, out_specs=out_specs, check_vma=False)
```

profile of v0, /device:TPU:1, one launch (start us, length us, event | category | flops | bytes accessed | tf_op | source)
XLA Modules:
  0.0 436.1 jit_solution(14999547283841224572)
XLA Ops:
  7.2 0.0 copy-start
  7.2 0.0 all-reduce.2.cloned.1.call-start
  7.2 0.9 slice.42
  8.1 4.9 %collective-permute-start = (bf16[9,640]{1,0:T(8,128)(2,1)S(1)}, bf16[9,640]{1,0:T(8,128)(2,1)S(1)}, u32[]{:S(2)}, u32[]{:S(2)}) collective-permute-start(bf16[9,640]{1,0:T(8,128)(2,1)S(1)} %slice.42), channel_id=1, source_target_pairs={{0,4},{4,8},{8,12},{12,16},{16,20},{20,24},{24,28},{28,32},{32,36}... | collective-permute-start | bytes 34568 | tf_op jit(solution)/shard_map/ppermute | solution.py:16
  13.0 0.9 slice_reduce_fusion.3
  13.9 1.5 convert_element_type.17
  15.4 0.0 collective-permute-done
  15.5 0.0 copy-start.10
  15.5 2.1 fusion.2
  17.6 1.9 collective-permute-start.1
  19.5 3.4 collective-permute-done.1
  22.9 0.0 copy-done
  22.9 6.8 %convolution_bitcast_fusion = f32[1280,1024]{0,1:T(8,128)} fusion(bf16[1280,640]{1,0:T(8,128)(2,1)S(1)} %copy-done, bf16[1024,640]{1,0:T(8,128)(2,1)S(1)} %copy-done.2, f32[9,640]{1,0:T(8,128)S(1)} %collective-permute-done.1, f32[1024,640]{1,0:T(8,128)S(1)} %fusion.2, f32[640]{0:T(1024)S(1)} %get-tuple-element.23, f32[640]{0:T(1024)S(1)} %get-tuple-element.24, ...), kind=kOutput, calls=%fused_computation.5 | convolution fusion | flops 1686896640 | bytes 10850816 | tf_op jit(solution)/shard_map/dot_general | solution.py:67
  29.7 0.0 all-reduce.2.cloned.1.call-update
  29.7 0.7 copy-done.4
  30.4 0.3 iota_compare_fusion
  30.7 1.9 convert_reduce_fusion
  32.6 0.1 multiply_reduce_fusion.1
  32.7 0.1 and_reduce_fusion.1
  32.9 8.1 %scatter_custom_fusion = s32[8192]{0:T(1024)S(1)} fusion(s32[2048]{0:T(1024)S(1)} %get-tuple-element.29, s32[2048]{0:T(1024)S(1)} %get-tuple-element.28, s32[]{:T(128)} %constant.19.clone.1), kind=kCustom, calls=%fused_computation.60 | custom fusion | bytes 32772
  41.0 0.1 reshape.86
  41.1 0.1 copy.147
  41.1 0.7 reshape.147
  41.8 11.6 %all-to-all-start = ((s32[64,1,128]{2,1,0:T(1,128)}), s32[64,1,128]{2,1,0:T(1,128)S(1)}, u32[]{:S(2)}, u32[]{:S(2)}) async-start(s32[64,1,128]{2,1,0:T(1,128)} %reshape.147), calls=%async_computation | async-start | bytes 65536 | tf_op jit(solution)/shard_map/all_to_all | solution.py:93
  53.5 93.5 %all-reduce.2.cloned.1.call-done = f32[1280,1024]{0,1:T(8,128)} async-done(((f32[1280,1024]{0,1:T(8,128)}), f32[1280,1024]{0,1:T(8,128)}) %all-reduce.2.cloned.1.call-update) | async-done | bytes 5242896 | tf_op jit(solution)/shard_map/psum | solution.py:70
  146.9 2.1 constant_dynamic-slice_fusion
  149.0 0.5 copy.100
  149.5 1.8 copy.116
  151.3 13.2 %scatter_custom_fusion.2 = f32[8192,160]{1,0:T(8,128)} fusion(s32[2048]{0:T(1024)S(1)} %get-tuple-element.29, f32[2048,160]{1,0:T(8,128)} %bitcast.36, f32[]{:T(128)} %constant.26.clone.1), kind=kCustom, calls=%fused_computation.6 | custom fusion | bytes 5243392
  164.5 7.7 %copy.104 = f32[2,64,64,160]{3,2,0,1:T(8,128)} copy(f32[2,64,64,160]{3,2,1,0:T(8,128)} %bitcast.32) | data formatting | bytes 10485760 | tf_op jit(solution)/shard_map/reshape | solution.py:90
  172.2 0.0 all-to-all-done
  172.2 11.2 %all-to-all-start.1 = ((f32[2,64,64,160]{3,2,0,1:T(8,128)}), f32[2,64,64,160]{3,2,0,1:T(8,128)}, u32[]{:S(2)}, u32[]{:S(2)}) async-start(f32[2,64,64,160]{3,2,0,1:T(8,128)} %copy.104), calls=%async_computation.1 | async-start | bytes 16777216 | tf_op jit(solution)/shard_map/all_to_all | solution.py:92
  183.4 0.5 broadcast.188
  183.9 0.7 reduce.20
  184.6 0.1 reshape.148
  184.7 0.1 sub.12
  184.9 0.1 multiply_reduce_fusion
  185.0 0.1 and_reduce_fusion
  185.2 44.3 %scatter_custom_fusion.1 = s32[1024]{0:T(1024)S(1)} fusion(s32[8192]{0:T(1024)S(1)} %bitcast.40, s32[8192]{0:T(1024)S(1)} %broadcast.161, s32[]{:T(128)} %constant.19.clone.1), kind=kCustom, calls=%fused_computation.74 | custom fusion | flops 8192 | bytes 4100
  229.5 139.6 %all-to-all-done.1 = f32[2,64,64,160]{3,2,0,1:T(8,128)} async-done(((f32[2,64,64,160]{3,2,0,1:T(8,128)}), f32[2,64,64,160]{3,2,0,1:T(8,128)}, u32[]{:S(2)}, u32[]{:S(2)}) %all-to-all-start.1) | async-done | bytes 5242912 | tf_op jit(solution)/shard_map/all_to_all | solution.py:92
  369.1 7.7 %copy.119 = f32[2,64,64,160]{3,2,1,0:T(8,128)} copy(f32[2,64,64,160]{3,2,0,1:T(8,128)} %all-to-all-done.1) | data formatting | bytes 10485760 | tf_op jit(solution)/shard_map/reshape | solution.py:96
  376.8 44.9 %scatter_custom_fusion.3 = f32[1024,160]{1,0:T(8,128)S(1)} fusion(s32[8192]{0:T(1024)S(1)} %bitcast.41, f32[8192,160]{1,0:T(8,128)} %bitcast.33, f32[]{:T(128)} %constant.26.clone.1), kind=kCustom, calls=%fused_computation.48 | custom fusion | flops 1310720 | bytes 655872
  421.7 0.6 copy.120
  422.3 0.0 copy-start.1
  422.3 4.0 broadcast_select_fusion
  426.4 1.0 copy.113
  427.3 1.0 copy.114
  428.3 1.0 copy.115
  (33 shorter events, 0.2 us)
Async XLA Ops:
  7.2 15.8 %copy-start = (bf16[1280,640]{1,0:T(8,128)(2,1)S(1)}, bf16[1280,640]{1,0:T(8,128)(2,1)}, u32[]{:S(2)}) copy-start(bf16[1280,640]{1,0:T(8,128)(2,1)} %param.14) | copy-start | bytes 4915204
  7.2 8.3 %copy-start.2 = (bf16[1024,640]{1,0:T(8,128)(2,1)S(1)}, bf16[1024,640]{1,0:T(8,128)(2,1)}, u32[]{:S(2)}) copy-start(bf16[1024,640]{1,0:T(8,128)(2,1)} %param.10) | copy-start | bytes 3932164
  7.2 139.7 %all-reduce.2.cloned.1.call-start = ((), (), s32[]{:S(2)}) async-start(), calls=%async_computation.2 | async-start | bytes 10485760 | tf_op jit(solution)/shard_map/psum | solution.py:70
  8.1 7.3 %collective-permute-start = (bf16[9,640]{1,0:T(8,128)(2,1)S(1)}, bf16[9,640]{1,0:T(8,128)(2,1)S(1)}, u32[]{:S(2)}, u32[]{:S(2)}) collective-permute-start(bf16[9,640]{1,0:T(8,128)(2,1)S(1)} %slice.42), channel_id=1, source_target_pairs={{0,4},{4,8},{8,12},{12,16},{16,20},{20,24},{24,28},{28,32},{32,36}... | collective-permute-start | bytes 34568 | tf_op jit(solution)/shard_map/ppermute | solution.py:16
  15.5 7.5 %copy-start.10 = (f32[1024]{0:T(1024)S(1)}, f32[1024]{0:T(1024)}, u32[]{:S(2)}) copy-start(f32[1024]{0:T(1024)} %param.12) | copy-start | bytes 12292
  17.6 5.3 %collective-permute-start.1 = (f32[9,640]{1,0:T(8,128)S(1)}, f32[9,640]{1,0:T(8,128)S(1)}, u32[]{:S(2)}, u32[]{:S(2)}) collective-permute-start(f32[9,640]{1,0:T(8,128)S(1)} %slice.56), channel_id=1, source_target_pairs={{4,0},{8,4},{12,8},{16,12},{20,16},{24,20},{28,24},{32,28},{36,32}... | collective-permute-start | bytes 69128 | tf_op jit(solution)/shard_map/ppermute | solution.py:16
  29.7 0.7 copy-start.4
  29.7 2.9 copy-start.8
  29.7 3.0 copy-start.9
  29.7 3.1 copy-start.5
  41.8 130.3 %all-to-all-start = ((s32[64,1,128]{2,1,0:T(1,128)}), s32[64,1,128]{2,1,0:T(1,128)S(1)}, u32[]{:S(2)}, u32[]{:S(2)}) async-start(s32[64,1,128]{2,1,0:T(1,128)} %reshape.147), calls=%async_computation | async-start | bytes 65536 | tf_op jit(solution)/shard_map/all_to_all | solution.py:93
  172.2 12.7 %copy-start.7 = (s32[2]{0:T(128)S(1)}, s32[2]{0:T(128)}, u32[]{:S(2)}) copy-start(s32[2]{0:T(128)} %constant.63) | copy-start | bytes 28
  172.2 12.8 %copy-start.6 = (s32[2]{0:T(128)S(1)}, s32[2]{0:T(128)}, u32[]{:S(2)}) copy-start(s32[2]{0:T(128)} %constant.66) | copy-start | bytes 28
  172.2 196.9 %all-to-all-start.1 = ((f32[2,64,64,160]{3,2,0,1:T(8,128)}), f32[2,64,64,160]{3,2,0,1:T(8,128)}, u32[]{:S(2)}, u32[]{:S(2)}) async-start(f32[2,64,64,160]{3,2,0,1:T(8,128)} %copy.104), calls=%async_computation.1 | async-start | bytes 16777216 | tf_op jit(solution)/shard_map/all_to_all | solution.py:92
  376.8 45.5 %copy-start.3 = (f32[2,512,160]{1,2,0:T(8,128)S(1)}, f32[2,512,160]{1,2,0:T(8,128)}, u32[]{:S(2)}) copy-start(f32[2,512,160]{1,2,0:T(8,128)} %param.19) | copy-start | bytes 1966084
  422.3 6.9 %copy-start.1 = (bf16[1280,640]{1,0:T(8,128)(2,1)S(1)}, bf16[1280,640]{1,0:T(8,128)(2,1)}, u32[]{:S(2)}) copy-start(bf16[1280,640]{1,0:T(8,128)(2,1)} %param.14) | copy-start | bytes 4915204
Sparse Core Ops, SparseCore 0:
  29.9 117.0 all-reduce.1
where the time goes:
time: 437 us; the launch traced here: 436 us
  waiting for transfers between devices  236 us (54%)
  other arithmetic  100 us (23%)
  local copies, waits for them, and re-layouts  48.5 us (11%)
  starting transfers between devices  29.7 us (7%)
  between operations  14.4 us (3%)
  matrix products  6.78 us (2%)
    all_to_all x1, waiting for transfers between devices, shards(): lax.all_to_all(send_grad, 'seq', split_axis=1, concat_axis=1, tiled=True)  140 us
    psum x1, waiting for transfers between devices, shards(): summed = lax.psum(full_term, 'tab')  93.5 us
    unnamed x9, other arithmetic  89.7 us
    unnamed x32, local copies, waits for them, and re-layouts  25.7 us
    all_to_all x1, starting transfers between devices, shards(): lax.all_to_all(send_rows, 'seq', split_axis=1, concat_axis=1, tiled=True)  11.6 us
    all_to_all x1, starting transfers between devices, shards(): lax.all_to_all(send_grad, 'seq', split_axis=1, concat_axis=1, tiled=True)  11.2 us
  transfers between devices with their start and end apart: 5, of which 3 were waited for; matrix products, arithmetic and copies ran while one was open for 19% of the time, Pallas kernels for 0%

commit v1 on v0

--- a/solution.py
+++ b/solution.py
@@ -8,6 +8,14 @@
 learn_rate = 0.01
 adam_steps = 10.0
 epsilon = 1e-08
+
+
+def sum_by_hops(x, name):
+    size, acc = (lax.axis_size(name), x)
+    for far in [1 << k for k in range(size.bit_length() - 1)]:
+        swap = [(i, i ^ far) for i in range(size)]
+        acc = acc + lax.ppermute(acc, name, swap)
+    return acc
 
 
 def from_behind(block, axis, distance):
@@ -67,7 +75,7 @@
     full_term = lax.dot_general(
         value_weight, scaled, (((1,), (1,)), ((), ())), preferred_element_type=jnp.float32
     )
-    summed = lax.psum(full_term, "tab")
+    summed = sum_by_hops(full_term, "tab")
     memory_grad = lax.dynamic_slice_in_dim(summed, lax.axis_index("tab") * own_width, own_width, 0)
     heads_grad = jnp.swapaxes(memory_grad.reshape(head_local, head_dim, length), 1, 2)
     owners = owner_ids[:, :, 0]

time: 437 us -> 538 us (1.23)
  waiting for transfers between devices: 236 us -> 343 us
  between operations: 14.4 us -> 1.02 us
  starting transfers between devices: 29.7 us -> 37.9 us
  other arithmetic: 100 us -> 106 us
    ppermute x0 -> x2, waiting for transfers between devices: none -> 200 us  [sum_by_hops(): acc = acc + lax.ppermute(acc, name, swap)]
    psum x1 -> x0, waiting for transfers between devices: 93.5 us -> none  [shards(): summed = lax.psum(full_term, 'tab')]
    add x0 -> x2, other arithmetic: none -> 6.06 us  [sum_by_hops(): acc = acc + lax.ppermute(acc, name, swap)]
  transfers between devices with their start and end apart: 5 -> 6, of which waited for: 3 -> 4; matrix products, arithmetic and copies ran while one was open for 19% -> 16% of each run, Pallas kernels for 0% -> 0%
where the time goes in v1:
time: 538 us
  waiting for transfers between devices  343 us (64%)
  other arithmetic  106 us (20%)
  local copies, waits for them, and re-layouts  45.8 us (9%)
  starting transfers between devices  37.9 us (7%)
    ppermute x2, waiting for transfers between devices, sum_by_hops(): acc = acc + lax.ppermute(acc, name, swap)  200 us
    all_to_all x1, waiting for transfers between devices, shards(): lax.all_to_all(send_grad, 'seq', split_axis=1, concat_axis=1, tiled=True)  140 us
    unnamed x9, other arithmetic  89.7 us
    unnamed x32, local copies, waits for them, and re-layouts  25 us
    all_to_all x1, starting transfers between devices, shards(): lax.all_to_all(send_grad, 'seq', split_axis=1, concat_axis=1, tiled=True)  13.6 us
    all_to_all x1, starting transfers between devices, shards(): lax.all_to_all(send_rows, 'seq', split_axis=1, concat_axis=1, tiled=True)  13.5 us
  transfers between devices with their start and end apart: 6, of which 4 were waited for; matrix products, arithmetic and copies ran while one was open for 16% of the time, Pallas kernels for 0%

profile of v1, /device:TPU:1, one launch (start us, length us, event | category | flops | bytes accessed | tf_op | source)
XLA Modules:
  0.0 537.6 jit_solution(14365454713520325662)
XLA Ops:
  0.6 0.0 copy-start
  0.7 0.9 slice.42
  1.5 4.9 collective-permute-start
  6.5 0.9 slice_reduce_fusion.3
  7.4 1.5 convert_element_type.17
  8.9 0.0 copy-start.10
  8.9 2.1 fusion.2
  11.0 1.9 collective-permute-start.1
  12.9 3.4 collective-permute-done.1
  16.3 3.4 convolution_bitcast_fusion
  19.7 0.0 copy-start.8
  19.7 0.0 copy-start.9
  19.7 0.0 copy-start.5
  19.7 1.3 collective-permute-start.2
  21.0 111.8 %collective-permute-done.2 = f32[1280,1024]{0,1:T(8,128)S(1)} collective-permute-done((f32[1280,1024]{0,1:T(8,128)S(1)}, f32[1280,1024]{0,1:T(8,128)S(1)}, u32[]{:S(2)}, u32[]{:S(2)}) %collective-permute-start.2) | collective-permute-done | bytes 5242912 | tf_op jit(solution)/shard_map/ppermute | solution.py:17
  132.9 3.0 add.107
  135.8 2.7 collective-permute-start.3
  138.6 0.3 iota_compare_fusion
  138.9 1.9 convert_reduce_fusion
  140.8 0.1 multiply_reduce_fusion.1
  140.9 0.1 and_reduce_fusion.1
  141.0 8.1 %scatter_custom_fusion = s32[8192]{0:T(1024)S(1)} fusion(s32[2048]{0:T(1024)S(1)} %get-tuple-element.29, s32[2048]{0:T(1024)S(1)} %get-tuple-element.28, s32[]{:T(128)} %constant.19.clone.1), kind=kCustom, calls=%fused_computation.61 | custom fusion | bytes 32772
  149.1 0.1 reshape.86
  149.2 0.1 copy.147
  149.3 0.7 reshape.147
  150.0 13.5 %all-to-all-start = ((s32[64,1,128]{2,1,0:T(1,128)}), s32[64,1,128]{2,1,0:T(1,128)S(1)}, u32[]{:S(2)}, u32[]{:S(2)}) async-start(s32[64,1,128]{2,1,0:T(1,128)} %reshape.147), calls=%async_computation | async-start | bytes 65536 | tf_op jit(solution)/shard_map/all_to_all | solution.py:101
  163.5 88.3 %collective-permute-done.3 = f32[1280,1024]{0,1:T(8,128)} collective-permute-done((f32[1280,1024]{0,1:T(8,128)}, f32[1280,1024]{0,1:T(8,128)}, u32[]{:S(2)}, u32[]{:S(2)}) %collective-permute-start.3) | collective-permute-done | bytes 5242912 | tf_op jit(solution)/shard_map/ppermute | solution.py:17
  251.8 3.1 dynamic-slice_add_fusion
  254.9 0.4 copy.100
  255.4 1.8 copy.116
  257.2 13.2 %scatter_custom_fusion.2 = f32[8192,160]{1,0:T(8,128)} fusion(s32[2048]{0:T(1024)S(1)} %get-tuple-element.29, f32[2048,160]{1,0:T(8,128)} %bitcast.36, f32[]{:T(128)} %constant.26.clone.1), kind=kCustom, calls=%fused_computation.6 | custom fusion | bytes 5243392
  270.4 7.7 %copy.104 = f32[2,64,64,160]{3,2,0,1:T(8,128)} copy(f32[2,64,64,160]{3,2,1,0:T(8,128)} %bitcast.32) | data formatting | bytes 10485760 | tf_op jit(solution)/shard_map/reshape | solution.py:98
  278.1 13.6 %all-to-all-start.1 = ((f32[2,64,64,160]{3,2,0,1:T(8,128)}), f32[2,64,64,160]{3,2,0,1:T(8,128)}, u32[]{:S(2)}, u32[]{:S(2)}) async-start(f32[2,64,64,160]{3,2,0,1:T(8,128)} %copy.104), calls=%async_computation.1 | async-start | bytes 16777216 | tf_op jit(solution)/shard_map/all_to_all | solution.py:100
  291.7 0.5 broadcast.188
  292.2 0.7 reduce.20
  293.0 0.1 reshape.148
  293.1 0.1 sub.12
  293.2 0.1 multiply_reduce_fusion
  293.3 0.1 and_reduce_fusion
  293.5 44.3 %scatter_custom_fusion.1 = s32[1024]{0:T(1024)S(1)} fusion(s32[8192]{0:T(1024)S(1)} %bitcast.40, s32[8192]{0:T(1024)S(1)} %broadcast.161, s32[]{:T(128)} %constant.19.clone.1), kind=kCustom, calls=%fused_computation.75 | custom fusion | flops 8192 | bytes 4100
  337.9 139.6 %all-to-all-done.1 = f32[2,64,64,160]{3,2,0,1:T(8,128)} async-done(((f32[2,64,64,160]{3,2,0,1:T(8,128)}), f32[2,64,64,160]{3,2,0,1:T(8,128)}, u32[]{:S(2)}, u32[]{:S(2)}) %all-to-all-start.1) | async-done | bytes 5242912 | tf_op jit(solution)/shard_map/all_to_all | solution.py:100
  477.4 7.7 %copy.119 = f32[2,64,64,160]{3,2,1,0:T(8,128)} copy(f32[2,64,64,160]{3,2,0,1:T(8,128)} %all-to-all-done.1) | data formatting | bytes 10485760 | tf_op jit(solution)/shard_map/reshape | solution.py:104
  485.2 44.9 %scatter_custom_fusion.3 = f32[1024,160]{1,0:T(8,128)S(1)} fusion(s32[8192]{0:T(1024)S(1)} %bitcast.41, f32[8192,160]{1,0:T(8,128)} %bitcast.33, f32[]{:T(128)} %constant.26.clone.1), kind=kCustom, calls=%fused_computation.49 | custom fusion | flops 1310720 | bytes 655872
  530.1 0.6 copy.120
  530.6 4.0 broadcast_select_fusion
  534.7 1.0 copy.113
  535.7 1.0 copy.114
  536.6 1.0 copy.115
  (35 shorter events, 0.2 us)
Async XLA Ops:
  0.6 15.7 %copy-start = (bf16[1280,640]{1,0:T(8,128)(2,1)S(1)}, bf16[1280,640]{1,0:T(8,128)(2,1)}, u32[]{:S(2)}) copy-start(bf16[1280,640]{1,0:T(8,128)(2,1)} %param.14) | copy-start | bytes 4915204
  0.6 8.2 %copy-start.2 = (bf16[1024,640]{1,0:T(8,128)(2,1)S(1)}, bf16[1024,640]{1,0:T(8,128)(2,1)}, u32[]{:S(2)}) copy-start(bf16[1024,640]{1,0:T(8,128)(2,1)} %param.10) | copy-start | bytes 3932164
  1.5 7.3 %collective-permute-start = (bf16[9,640]{1,0:T(8,128)(2,1)S(1)}, bf16[9,640]{1,0:T(8,128)(2,1)S(1)}, u32[]{:S(2)}, u32[]{:S(2)}) collective-permute-start(bf16[9,640]{1,0:T(8,128)(2,1)S(1)} %slice.42), channel_id=1, source_target_pairs={{0,4},{4,8},{8,12},{12,16},{16,20},{20,24},{24,28},{28,32},{32,36}... | collective-permute-start | bytes 34568 | tf_op jit(solution)/shard_map/ppermute | solution.py:24
  8.9 7.4 %copy-start.10 = (f32[1024]{0:T(1024)S(1)}, f32[1024]{0:T(1024)}, u32[]{:S(2)}) copy-start(f32[1024]{0:T(1024)} %param.12) | copy-start | bytes 12292
  11.0 5.3 collective-permute-start.1
  19.7 118.9 %copy-start.4 = (s32[2,1024,1]{1,2,0:T(1,128)S(1)}, s32[2,1024,1]{1,2,0:T(1,128)}, u32[]{:S(2)}) copy-start(s32[2,1024,1]{1,2,0:T(1,128)} %param.15) | copy-start | bytes 24580
  19.7 121.1 %copy-start.8 = (s32[2]{0:T(128)S(1)}, s32[2]{0:T(128)}, u32[]{:S(2)}) copy-start(s32[2]{0:T(128)} %constant.57) | copy-start | bytes 28
  19.7 121.2 %copy-start.9 = (s32[2]{0:T(128)S(1)}, s32[2]{0:T(128)}, u32[]{:S(2)}) copy-start(s32[2]{0:T(128)} %constant.60) | copy-start | bytes 28
  19.7 121.3 %copy-start.5 = (s32[2,1024]{1,0:T(2,128)S(1)}, s32[2,1024]{1,0:T(2,128)}, u32[]{:S(2)}) copy-start(s32[2,1024]{1,0:T(2,128)} %param.16) | copy-start | bytes 24580
  19.7 113.1 %collective-permute-start.2 = (f32[1280,1024]{0,1:T(8,128)S(1)}, f32[1280,1024]{0,1:T(8,128)S(1)}, u32[]{:S(2)}, u32[]{:S(2)}) collective-permute-start(f32[1280,1024]{0,1:T(8,128)S(1)} %convolution_bitcast_fusion), channel_id=1, source_target_pairs={{0,1},{1,0},{2,3},{3,2},{4,5},{5,4},{6,7},{7,6},{8,9},{9,8},{10,11... | collective-permute-start | bytes 15728648 | tf_op jit(solution)/shard_map/ppermute | solution.py:17
  135.8 116.0 %collective-permute-start.3 = (f32[1280,1024]{0,1:T(8,128)}, f32[1280,1024]{0,1:T(8,128)}, u32[]{:S(2)}, u32[]{:S(2)}) collective-permute-start(f32[1280,1024]{0,1:T(8,128)} %add.107), channel_id=1, source_target_pairs={{0,2},{1,3},{2,0},{3,1},{4,6},{5,7},{6,4},{7,5},{8,10},{9,11},{10,... | collective-permute-start | bytes 15728648 | tf_op jit(solution)/shard_map/ppermute | solution.py:17
  150.0 128.1 %all-to-all-start = ((s32[64,1,128]{2,1,0:T(1,128)}), s32[64,1,128]{2,1,0:T(1,128)S(1)}, u32[]{:S(2)}, u32[]{:S(2)}) async-start(s32[64,1,128]{2,1,0:T(1,128)} %reshape.147), calls=%async_computation | async-start | bytes 65536 | tf_op jit(solution)/shard_map/all_to_all | solution.py:101
  278.1 15.1 %copy-start.7 = (s32[2]{0:T(128)S(1)}, s32[2]{0:T(128)}, u32[]{:S(2)}) copy-start(s32[2]{0:T(128)} %constant.63) | copy-start | bytes 28
  278.1 15.2 %copy-start.6 = (s32[2]{0:T(128)S(1)}, s32[2]{0:T(128)}, u32[]{:S(2)}) copy-start(s32[2]{0:T(128)} %constant.66) | copy-start | bytes 28
  278.1 199.3 %all-to-all-start.1 = ((f32[2,64,64,160]{3,2,0,1:T(8,128)}), f32[2,64,64,160]{3,2,0,1:T(8,128)}, u32[]{:S(2)}, u32[]{:S(2)}) async-start(f32[2,64,64,160]{3,2,0,1:T(8,128)} %copy.104), calls=%async_computation.1 | async-start | bytes 16777216 | tf_op jit(solution)/shard_map/all_to_all | solution.py:100
  485.2 45.5 %copy-start.3 = (f32[2,512,160]{1,2,0:T(8,128)S(1)}, f32[2,512,160]{1,2,0:T(8,128)}, u32[]{:S(2)}) copy-start(f32[2,512,160]{1,2,0:T(8,128)} %param.19) | copy-start | bytes 1966084
  530.6 6.9 %copy-start.1 = (bf16[1280,640]{1,0:T(8,128)(2,1)S(1)}, bf16[1280,640]{1,0:T(8,128)(2,1)}, u32[]{:S(2)}) copy-start(bf16[1280,640]{1,0:T(8,128)(2,1)} %param.14) | copy-start | bytes 4915204
